TPU v7x, 128 devices: a whole 4x4x4 slice. The times are simulated.
128 devices in a mesh: fer: 8 (over z, y_hi), bos: 16 (over y_lo, x, core).
Axes of the slice: x: 4, y: 4 (y_hi: 2, y_lo: 2; y = y_hi * 2 + y_lo), z: 4, core: 2. Of those that a mesh axis runs over, the one named last changes fastest.
Arguments:
- green: bfloat16 [4, 64, 9, 64, 128], P(None, 'fer', None, 'bos'), may hold values from -6 to 6
- bos_weight: bfloat16 [128, 9, 64, 128], P('bos'), may hold values from -12 to 12
- vertex: float32 [64, 128], P('fer', 'bos'), may hold values from 0.25 to 1.75
- block_order: int32 [16], replicated, may hold values from 0 to 15, each once
- window_start: int32 [1], replicated, may hold values from 0 to 64
Outputs:
- sigma: float32 [64, 64, 9, 128], P('bos', 'fer')
Inputs may be any that keep to these rules, and one draw needn't show every extreme that they name: block_order holds every block number once.
All inputs are finite; a program needn't handle non-finite values.
Results may differ from a plain program's by a relative error of at most 0.0003.
Values may be sent and summed in bfloat16 or wider, within the bound.
A program may use at most 128 MiB of HBM per device.

v0:
```python
import math
import jax
import jax.numpy as jnp
from jax import lax
from jax.sharding import PartitionSpec as P

HIGHEST = lax.Precision.HIGHEST


def passed_along(array, axis, by):
    size = lax.axis_size(axis)
    return lax.ppermute(array, axis, [(i, (i + by) % size) for i in range(size)])


def trig_tables(length):
    index = jnp.arange(length, dtype=jnp.int32)
    phase = (index[:, None] * index[None, :] % length).astype(jnp.float32) * (
        2.0 * math.pi / length
    )
    return (jnp.cos(phase), jnp.sin(phase))


def row_matrix(length, forward):
    cosine, sine = trig_tables(length)
    if forward:
        upper = jnp.concatenate([cosine, -sine], axis=1)
        lower = jnp.concatenate([sine, cosine], axis=1)
        block = jnp.concatenate([upper, lower], axis=0)
    else:
        upper = jnp.concatenate([cosine, sine], axis=1)
        lower = jnp.concatenate([-sine, cosine], axis=1)
        block = jnp.concatenate([upper, lower], axis=0) / length
    turned = jnp.concatenate([block[:, length:], -block[:, :length]], axis=1)
    return jnp.concatenate([block, turned], axis=1)


def col_tables(length, forward):
    cosine, sine = trig_tables(length)
    if forward:
        return (cosine, sine)
    return (cosine / length, -sine / length)


def row_step(field, matrix):
    return jnp.einsum("...c,cd->...d", field, matrix, precision=HIGHEST)


def col_step(halves, cos_part, sin_part):
    width = halves.shape[-1] // 2
    first = jnp.einsum("ax,nmxc->nmac", cos_part, halves[..., :width], precision=HIGHEST)
    return first + jnp.einsum("ax,nmxc->nmac", sin_part, halves[..., width:], precision=HIGHEST)


def body(green, bos_weight, vertex, block_order, window_start):
    num_fer = lax.axis_size("fer")
    fer_index = lax.axis_index("fer")
    bos_index = lax.axis_index("bos")
    num_slot = green.shape[0]
    window_dev = green.shape[1]
    orbitals = int(round(math.sqrt(green.shape[2])))
    bos_dev = bos_weight.shape[0]
    rows_all = bos_weight.shape[2]
    half_width = bos_weight.shape[3] // 2
    block_id = lax.dynamic_index_in_dim(block_order, bos_index, 0, keepdims=False)
    offset = window_start[0] + block_id * bos_dev
    shift_blocks = offset // window_dev
    inner = offset % window_dev
    shift_bits = shift_blocks % num_fer
    forward_rows = row_matrix(half_width, True)
    inverse_rows = row_matrix(half_width, False)
    forward_cos, forward_sin = col_tables(rows_all, True)
    inverse_cos, inverse_sin = col_tables(rows_all, False)
    full_rows = lax.all_gather(green, "bos", axis=3, tiled=True)
    current = full_rows
    for level in range(num_fer.bit_length() - 1):
        moved = passed_along(current, "fer", -(1 << level))
        current = jnp.where((shift_bits >> level) % 2 == 1, moved, current)
    sources = [current]
    for extra in range(2):
        current = passed_along(current, "fer", -1)
        sources.append(current)
    picked = []
    for extra in range(3):
        slot = (fer_index + shift_blocks + extra) // num_fer % num_slot
        picked.append(lax.dynamic_index_in_dim(sources[extra], slot, 0, keepdims=False))
    blocks = jnp.concatenate(picked, axis=0)
    halves = row_step(blocks.astype(jnp.float32), forward_rows)
    green_real = col_step(halves, forward_cos, forward_sin)
    weight_real = col_step(
        row_step(bos_weight.astype(jnp.float32), inverse_rows), inverse_cos, inverse_sin
    )
    total = jnp.zeros((window_dev, orbitals * orbitals, rows_all, 2 * half_width), jnp.float32)
    for column in range(bos_dev):
        part = lax.dynamic_slice_in_dim(green_real, inner + column, window_dev, 0)
        part = part.reshape(window_dev, orbitals, orbitals, 1, rows_all, 2 * half_width)
        factor = weight_real[column].reshape(1, 1, orbitals, orbitals, rows_all, 2 * half_width)
        green_re, green_im = (part[..., :half_width], part[..., half_width:])
        weight_re, weight_im = (factor[..., :half_width], factor[..., half_width:])
        real_part = jnp.sum(green_re * weight_re - green_im * weight_im, axis=2)
        imag_part = jnp.sum(green_re * weight_im + green_im * weight_re, axis=2)
        product = jnp.concatenate([real_part, imag_part], axis=-1)
        product = product.reshape(window_dev, orbitals * orbitals, rows_all, 2 * half_width)
        total = total + vertex[:, column][:, None, None, None] * product
    sigma_halves = row_step(-total, inverse_rows)
    width = sigma_halves.shape[-1] // 2
    first = jnp.einsum("ax,nmxc->anmc", inverse_cos, sigma_halves[..., :width], precision=HIGHEST)
    return lax.psum_scatter(
        first
        + jnp.einsum("ax,nmxc->anmc", inverse_sin, sigma_halves[..., width:], precision=HIGHEST),
        "bos",
        scatter_dimension=0,
        tiled=True,
    )


def solution(mesh):
    return jax.shard_map(
        body,
        mesh=mesh,
        in_specs=(
            P(None, "fer", None, "bos", None),
            P("bos", None, None, None),
            P("fer", "bos"),
            P(),
            P(),
        ),
        out_specs=P("bos", "fer", None, None),
        check_vma=False,
    )
```

profile of v0, /device:TPU:0, one launch (start us, length us, event | category | flops | bytes accessed | tf_op | source)
XLA Modules:
  0.0 767.3 jit_solution(11547539962003725166)
XLA Ops:
  8.4 41.5 %all-gather.2.cloned.1.call-done = bf16[4,8,9,64,128]{4,1,2,0,3:T(8,128)(2,1)} async-done(((bf16[4,8,9,4,128]{4,1,2,0,3:T(8,128)(2,1)}), bf16[4,8,9,64,128]{4,1,2,0,3:T(8,128)(2,1)}) %all-gather.2.cloned.1.call-update) | async-done | bytes 4718608 | tf_op jit(solution)/shard_map/all_gather | solution.py:73
  50.0 5.1 collective-permute-start
  57.6 99.2 %collective-permute-done = bf16[4,8,9,64,128]{4,1,2,0,3:T(8,128)(2,1)} collective-permute-done((bf16[4,8,9,64,128]{4,1,2,0,3:T(8,128)(2,1)}, bf16[4,8,9,64,128]{4,1,2,0,3:T(8,128)(2,1)}, u32[]{:S(2)}, u32[]{:S(2)}) %collective-permute-start) | collective-permute-done | bytes 4718624 | tf_op jit(solution)/shard_map/ppermute | solution.py:12
  156.8 5.0 broadcast_select_fusion
  163.7 101.6 %collective-permute-done.1 = bf16[4,8,9,64,128]{4,1,2,0,3:T(8,128)(2,1)} collective-permute-done((bf16[4,8,9,64,128]{4,1,2,0,3:T(8,128)(2,1)}, bf16[4,8,9,64,128]{4,1,2,0,3:T(8,128)(2,1)}, u32[]{:S(2)}, u32[]{:S(2)}) %collective-permute-start.1) | collective-permute-done | bytes 4718624 | tf_op jit(solution)/shard_map/ppermute | solution.py:12
  265.2 5.0 broadcast_select_fusion.1
  272.3 102.0 %collective-permute-done.2 = bf16[4,8,9,64,128]{4,1,2,0,3:T(8,128)(2,1)} collective-permute-done((bf16[4,8,9,64,128]{4,1,2,0,3:T(8,128)(2,1)}, bf16[4,8,9,64,128]{4,1,2,0,3:T(8,128)(2,1)}, u32[]{:S(2)}, u32[]{:S(2)}) %collective-permute-start.2) | collective-permute-done | bytes 4718624 | tf_op jit(solution)/shard_map/ppermute | solution.py:12
  379.3 7.3 collective-permute-start.3
  386.6 98.8 %collective-permute-done.3 = bf16[4,8,9,64,128]{4,1,2,0,3:T(8,128)(2,1)} collective-permute-done((bf16[4,8,9,64,128]{4,1,2,0,3:T(8,128)(2,1)S(1)}, bf16[4,8,9,64,128]{4,1,2,0,3:T(8,128)(2,1)}, u32[]{:S(2)}, u32[]{:S(2)}) %collective-permute-start.3) | collective-permute-done | bytes 4718624 | tf_op jit(solution)/shard_map/ppermute | solution.py:12
  485.4 6.6 collective-permute-start.4
  510.5 79.8 %collective-permute-done.4 = bf16[4,8,9,64,128]{4,1,2,0,3:T(8,128)(2,1)} collective-permute-done((bf16[4,8,9,64,128]{4,1,2,0,3:T(8,128)(2,1)}, bf16[4,8,9,64,128]{4,1,2,0,3:T(8,128)(2,1)}, u32[]{:S(2)}, u32[]{:S(2)}) %collective-permute-start.4) | collective-permute-done | bytes 4718624 | tf_op jit(solution)/shard_map/ppermute | solution.py:12
  591.9 6.1 fusion.4
  598.0 5.0 copy-done.2
  603.1 7.3 fusion
  610.4 9.5 %fusion.10 = f32[24,9,128,64]{2,3,1,0:T(8,128)S(1)} fusion(f32[24,9,128,64]{2,3,1,0:T(8,128)S(1)} %fusion, f32[24,9,64,256]{3,2,1,0:T(8,128)} %copy-done.2), kind=kOutput, calls=%fused_computation.29 | convolution fusion | flops 1360781312 | bytes 21233664 | tf_op jit(solution)/shard_map/ax,nmxc->nmac/dot_general | solution.py:50
  619.9 4.7 constant_dynamic-slice_fusion.7
  624.6 4.8 slice_bitcast_fusion.15
  643.9 3.7 subtract_reduce_fusion.7
  655.1 3.3 subtract_reduce_fusion.5
  660.9 3.3 subtract_reduce_fusion.4
  665.9 3.5 subtract_reduce_fusion.3
  678.7 3.5 subtract_reduce_fusion
  683.1 4.8 fusion.21
  695.4 64.8 %reduce-scatter.2.cloned.1.call-done = f32[4,8,9,128]{3,1,2,0:T(8,128)} async-done(((f32[64,8,9,128]{3,1,2,0:T(8,128)}), f32[4,8,9,128]{3,1,2,0:T(8,128)}) %reduce-scatter.2.cloned.1.call-update) | async-done | bytes 147472 | tf_op jit(solution)/shard_map/reduce_scatter | solution.py:107
  (115 shorter events, 75.8 us)
Async XLA Ops:
  6.5 486.9 %copy-start = (bf16[8,9,64,128]{3,2,1,0:T(8,128)(2,1)S(1)}, bf16[8,9,64,128]{3,2,1,0:T(8,128)(2,1)}, u32[]{:S(2)}) copy-start(bf16[8,9,64,128]{3,2,1,0:T(8,128)(2,1)} %param.6) | copy-start | bytes 3538948
  6.5 43.4 %all-gather.2.cloned.1.call-start = ((), (), s32[]{:S(2)}) async-start(), calls=%async_computation.1 | async-start | bytes 5013504 | tf_op jit(solution)/shard_map/all_gather | solution.py:73
  8.4 751.9 %reduce-scatter.2.cloned.1.call-start = ((), (), s32[]{:S(2)}) async-start(), calls=%async_computation.2 | async-start | bytes 2506752 | tf_op jit(solution)/shard_map/reduce_scatter | solution.py:107
  50.0 106.8 %collective-permute-start = (bf16[4,8,9,64,128]{4,1,2,0,3:T(8,128)(2,1)}, bf16[4,8,9,64,128]{4,1,2,0,3:T(8,128)(2,1)}, u32[]{:S(2)}, u32[]{:S(2)}) collective-permute-start(bf16[4,8,9,64,128]{4,1,2,0,3:T(8,128)(2,1)} %all-gather.2.cloned.1.call-done), channel_id=1, source_target_pairs={{0,112},{16,0},{32,16},{48,32},{64,48},{80,64},{96,80},{112,96},{1... | collective-permute-start | bytes 14155784 | tf_op jit(solution)/shard_map/ppermute | solution.py:12
  161.8 103.4 %collective-permute-start.1 = (bf16[4,8,9,64,128]{4,1,2,0,3:T(8,128)(2,1)}, bf16[4,8,9,64,128]{4,1,2,0,3:T(8,128)(2,1)}, u32[]{:S(2)}, u32[]{:S(2)}) collective-permute-start(bf16[4,8,9,64,128]{4,1,2,0,3:T(8,128)(2,1)} %broadcast_select_fusion), channel_id=1, source_target_pairs={{0,96},{16,112},{32,0},{48,16},{64,32},{80,48},{96,64},{112,80},{1... | collective-permute-start | bytes 14155784 | tf_op jit(solution)/shard_map/ppermute | solution.py:12
  270.2 104.0 %collective-permute-start.2 = (bf16[4,8,9,64,128]{4,1,2,0,3:T(8,128)(2,1)}, bf16[4,8,9,64,128]{4,1,2,0,3:T(8,128)(2,1)}, u32[]{:S(2)}, u32[]{:S(2)}) collective-permute-start(bf16[4,8,9,64,128]{4,1,2,0,3:T(8,128)(2,1)} %broadcast_select_fusion.1), channel_id=1, source_target_pairs={{0,64},{16,80},{32,96},{48,112},{64,0},{80,16},{96,32},{112,48},{1... | collective-permute-start | bytes 14155784 | tf_op jit(solution)/shard_map/ppermute | solution.py:12
  272.3 219.8 %copy-start.29 = (f32[8,8]{1,0:T(8,128)S(1)}, f32[8,8]{1,0:T(8,128)}, u32[]{:S(2)}) copy-start(f32[8,8]{1,0:T(8,128)} %param.7) | copy-start | bytes 772
  377.1 2.2 copy-start.13
  379.3 106.1 %collective-permute-start.3 = (bf16[4,8,9,64,128]{4,1,2,0,3:T(8,128)(2,1)S(1)}, bf16[4,8,9,64,128]{4,1,2,0,3:T(8,128)(2,1)}, u32[]{:S(2)}, u32[]{:S(2)}) collective-permute-start(bf16[4,8,9,64,128]{4,1,2,0,3:T(8,128)(2,1)S(1)} %broadcast_select_fusion.2), channel_id=1, source_target_pairs={{0,112},{16,0},{32,16},{48,32},{64,48},{80,64},{96,80},{112,96},{1... | collective-permute-start | bytes 14155784 | tf_op jit(solution)/shard_map/ppermute | solution.py:12
  485.4 104.8 %collective-permute-start.4 = (bf16[4,8,9,64,128]{4,1,2,0,3:T(8,128)(2,1)}, bf16[4,8,9,64,128]{4,1,2,0,3:T(8,128)(2,1)}, u32[]{:S(2)}, u32[]{:S(2)}) collective-permute-start(bf16[4,8,9,64,128]{4,1,2,0,3:T(8,128)(2,1)} %collective-permute-done.3), channel_id=1, source_target_pairs={{0,112},{16,0},{32,16},{48,32},{64,48},{80,64},{96,80},{112,96},{1... | collective-permute-start | bytes 14155784 | tf_op jit(solution)/shard_map/ppermute | solution.py:12
  493.4 2.1 copy-start.27
  598.0 5.1 copy-start.2
  624.6 4.8 copy-start.5
  629.4 2.5 copy-start.4
  631.8 3.2 copy-start.3
  642.1 1.7 copy-start.26
  647.6 1.7 copy-start.24
  652.6 2.4 copy-start.10
  652.6 2.4 copy-start.21
  652.7 2.4 copy-start.22
  658.4 2.4 copy-start.8
  658.4 2.4 copy-start.19
  658.4 2.4 copy-start.20
  692.6 67.6 %copy-start.1 = (bf16[8,9,64,128]{3,2,1,0:T(8,128)(2,1)S(1)}, bf16[8,9,64,128]{3,2,1,0:T(8,128)(2,1)}, u32[]{:S(2)}) copy-start(bf16[8,9,64,128]{3,2,1,0:T(8,128)(2,1)} %param.6) | copy-start | bytes 3538948
  (14 other events, 19.7 us)
Sparse Core Ops, SparseCore 0:
  9.1 40.8 all-gather.1
  695.6 64.6 reduce-scatter.1
where the time goes:
time: 771 us; the launch traced here: 767 us
  waiting for transfers between devices  588 us (76%)
  local copies, waits for them, and re-layouts  55.9 us (7%)
  other arithmetic  45.9 us (6%)
  matrix products  39.4 us (5%)
  starting transfers between devices  23 us (3%)
  between operations  15.5 us (2%)
    ppermute x5, waiting for transfers between devices, passed_along(): lax.ppermute(array, axis, [(i, (i + by) % size) for i in range(size)])  481 us
    reduce_scatter x1, waiting for transfers between devices, body(): lax.psum_scatter(first + jnp.einsum('ax,nmxc->anmc', inverse_sin, sigma_h...  64.8 us
    all_gather x1, waiting for transfers between devices, body(): full_rows = lax.all_gather(green, 'bos', axis=3, tiled=True)  41.5 us
    reduce_sum x8, other arithmetic, body(): real_part = jnp.sum(green_re * weight_re - green_im * weight_im, axis=2)  27.1 us
    mul x16, local copies, waits for them, and re-layouts, body(): real_part = jnp.sum(green_re * weight_re - green_im * weight_im, axis=2)  24.8 us
    ppermute x5, starting transfers between devices, passed_along(): lax.ppermute(array, axis, [(i, (i + by) % size) for i in range(size)])  22.9 us
    unnamed x63, local copies, waits for them, and re-layouts  16.4 us
  transfers between devices with their start and end apart: 7, of which 7 were waited for; matrix products, arithmetic and copies ran while one was open for 3% of the time, Pallas kernels for 0%

commit v1 on v0

--- a/solution.py
+++ b/solution.py
@@ -70,7 +70,8 @@
     inverse_rows = row_matrix(half_width, False)
     forward_cos, forward_sin = col_tables(rows_all, True)
     inverse_cos, inverse_sin = col_tables(rows_all, False)
-    full_rows = lax.all_gather(green, "bos", axis=3, tiled=True)
+    sent = jnp.stack([green] * lax.axis_size("bos"))
+    full_rows = jnp.concatenate(lax.all_to_all(sent, "bos", 0, 0), axis=3)
     current = full_rows
     for level in range(num_fer.bit_length() - 1):
         moved = passed_along(current, "fer", -(1 << level))

time: 771 us -> 798 us (1.035)
  blocking collectives: 0 us -> 61.1 us
  waiting for transfers between devices: 588 us -> 548 us
    all_to_all x0 -> x1, blocking collectives: none -> 61.1 us  [body(): full_rows = jnp.concatenate(lax.all_to_all(sent, 'bos', 0, 0), axis=3)]
    all_gather x1 -> x0, waiting for transfers between devices: 41.5 us -> none  [body(): full_rows = lax.all_gather(green, 'bos', axis=3, tiled=True)]
    unnamed x63 -> x64, local copies, waits for them, and re-layouts: 16.4 us -> 14.6 us
  transfers between devices with their start and end apart: 7 -> 6, of which waited for: 7 -> 6; matrix products, arithmetic and copies ran while one was open for 3% -> 2% of each run, Pallas kernels for 0% -> 0%
where the time goes in v1:
time: 798 us; the launch traced here: 793 us
  waiting for transfers between devices  548 us (69%)
  blocking collectives  61.1 us (8%)
  local copies, waits for them, and re-layouts  59.7 us (7%)
  other arithmetic  45.8 us (6%)
  matrix products  39.4 us (5%)
  starting transfers between devices  23.5 us (3%)
  between operations  15.5 us (2%)
    ppermute x5, waiting for transfers between devices, passed_along(): lax.ppermute(array, axis, [(i, (i + by) % size) for i in range(size)])  478 us
    reduce_scatter x1, waiting for transfers between devices, body(): lax.psum_scatter(first + jnp.einsum('ax,nmxc->anmc', inverse_sin, sigma_h...  69.5 us
    all_to_all x1, blocking collectives, body(): full_rows = jnp.concatenate(lax.all_to_all(sent, 'bos', 0, 0), axis=3)  61.1 us
    reduce_sum x8, other arithmetic, body(): real_part = jnp.sum(green_re * weight_re - green_im * weight_im, axis=2)  27.1 us
    mul x16, local copies, waits for them, and re-layouts, body(): real_part = jnp.sum(green_re * weight_re - green_im * weight_im, axis=2)  24.8 us
    ppermute x5, starting transfers between devices, passed_along(): lax.ppermute(array, axis, [(i, (i + by) % size) for i in range(size)])  23.5 us
  transfers between devices with their start and end apart: 6, of which 6 were waited for; matrix products, arithmetic and copies ran while one was open for 2% of the time, Pallas kernels for 0%

profile of v1, /device:TPU:0, one launch (start us, length us, event | category | flops | bytes accessed | tf_op | source)
XLA Modules:
  0.0 792.8 jit_solution(11642520241592648476)
XLA Ops:
  9.4 61.1 %all_to_all.5 = bf16[16,4,8,9,4,128]{5,4,3,2,1,0:T(4,128)(2,1)S(1)} all-to-all(bf16[16,4,8,9,4,128]{5,4,3,2,1,0:T(4,128)(2,1)S(1)} %stack.2), channel_id=1, replica_groups=mesh['fer'=8,'bos'=16] {'bos'}, dimensions={0} | all-to-all | bytes 9437184 | tf_op jit(solution)/shard_map/all_to_all | solution.py:74
  70.5 3.5 copy.13
  74.0 6.4 collective-permute-start
  82.4 99.0 %collective-permute-done = bf16[4,8,9,64,128]{4,1,3,2,0:T(8,128)(2,1)} collective-permute-done((bf16[4,8,9,64,128]{4,1,3,2,0:T(8,128)(2,1)}, bf16[4,8,9,64,128]{4,1,3,2,0:T(8,128)(2,1)}, u32[]{:S(2)}, u32[]{:S(2)}) %collective-permute-start) | collective-permute-done | bytes 4718624 | tf_op jit(solution)/shard_map/ppermute | solution.py:12
  181.4 5.0 broadcast_select_fusion
  188.0 100.9 %collective-permute-done.1 = bf16[4,8,9,64,128]{4,1,3,2,0:T(8,128)(2,1)} collective-permute-done((bf16[4,8,9,64,128]{4,1,3,2,0:T(8,128)(2,1)}, bf16[4,8,9,64,128]{4,1,3,2,0:T(8,128)(2,1)}, u32[]{:S(2)}, u32[]{:S(2)}) %collective-permute-start.1) | collective-permute-done | bytes 4718624 | tf_op jit(solution)/shard_map/ppermute | solution.py:12
  288.9 4.9 broadcast_select_fusion.1
  295.3 101.6 %collective-permute-done.2 = bf16[4,8,9,64,128]{4,1,3,2,0:T(8,128)(2,1)} collective-permute-done((bf16[4,8,9,64,128]{4,1,3,2,0:T(8,128)(2,1)}, bf16[4,8,9,64,128]{4,1,3,2,0:T(8,128)(2,1)}, u32[]{:S(2)}, u32[]{:S(2)}) %collective-permute-start.2) | collective-permute-done | bytes 4718624 | tf_op jit(solution)/shard_map/ppermute | solution.py:12
  402.0 7.3 collective-permute-start.3
  409.3 97.9 %collective-permute-done.3 = bf16[4,8,9,64,128]{4,1,3,2,0:T(8,128)(2,1)} collective-permute-done((bf16[4,8,9,64,128]{4,1,3,2,0:T(8,128)(2,1)S(1)}, bf16[4,8,9,64,128]{4,1,3,2,0:T(8,128)(2,1)}, u32[]{:S(2)}, u32[]{:S(2)}) %collective-permute-start.3) | collective-permute-done | bytes 4718624 | tf_op jit(solution)/shard_map/ppermute | solution.py:12
  507.2 6.6 collective-permute-start.4
  532.2 78.9 %collective-permute-done.4 = bf16[4,8,9,64,128]{4,1,3,2,0:T(8,128)(2,1)} collective-permute-done((bf16[4,8,9,64,128]{4,1,3,2,0:T(8,128)(2,1)}, bf16[4,8,9,64,128]{4,1,3,2,0:T(8,128)(2,1)}, u32[]{:S(2)}, u32[]{:S(2)}) %collective-permute-start.4) | collective-permute-done | bytes 4718624 | tf_op jit(solution)/shard_map/ppermute | solution.py:12
  612.8 6.1 fusion.4
  618.9 5.0 copy-done.2
  623.9 7.3 fusion
  631.3 9.5 %fusion.10 = f32[24,9,128,64]{2,3,1,0:T(8,128)S(1)} fusion(f32[24,9,128,64]{2,3,1,0:T(8,128)S(1)} %fusion, f32[24,9,64,256]{3,2,1,0:T(8,128)} %copy-done.2), kind=kOutput, calls=%fused_computation.29 | convolution fusion | flops 1360781312 | bytes 21233664 | tf_op jit(solution)/shard_map/ax,nmxc->nmac/dot_general | solution.py:50
  640.7 4.7 constant_dynamic-slice_fusion.7
  645.5 4.8 slice_bitcast_fusion.15
  664.7 3.7 subtract_reduce_fusion.7
  670.2 3.3 subtract_reduce_fusion.6
  686.8 3.5 subtract_reduce_fusion.3
  699.6 3.5 subtract_reduce_fusion
  703.9 4.8 fusion.21
  716.3 69.5 %reduce-scatter.2.cloned.1.call-done = f32[4,8,9,128]{3,1,2,0:T(8,128)} async-done(((f32[64,8,9,128]{3,1,2,0:T(8,128)}), f32[4,8,9,128]{3,1,2,0:T(8,128)}) %reduce-scatter.2.cloned.1.call-update) | async-done | bytes 147472 | tf_op jit(solution)/shard_map/reduce_scatter | solution.py:108
  (116 shorter events, 78.5 us)
Async XLA Ops:
  6.5 508.6 %copy-start = (bf16[8,9,64,128]{3,2,1,0:T(8,128)(2,1)S(1)}, bf16[8,9,64,128]{3,2,1,0:T(8,128)(2,1)}, u32[]{:S(2)}) copy-start(bf16[8,9,64,128]{3,2,1,0:T(8,128)(2,1)} %param.6) | copy-start | bytes 3538948
  6.5 779.2 %reduce-scatter.2.cloned.1.call-start = ((), (), s32[]{:S(2)}) async-start(), calls=%async_computation.2 | async-start | bytes 2506752 | tf_op jit(solution)/shard_map/reduce_scatter | solution.py:108
  70.5 10.5 %copy-start.31 = (s32[16]{0:T(128)S(1)}, s32[16]{0:T(128)}, u32[]{:S(2)}) copy-start(s32[16]{0:T(128)} %param.8) | copy-start | bytes 196
  74.0 107.4 %collective-permute-start = (bf16[4,8,9,64,128]{4,1,3,2,0:T(8,128)(2,1)}, bf16[4,8,9,64,128]{4,1,3,2,0:T(8,128)(2,1)}, u32[]{:S(2)}, u32[]{:S(2)}) collective-permute-start(bf16[4,8,9,64,128]{4,1,3,2,0:T(8,128)(2,1)} %bitcast.4), channel_id=1, source_target_pairs={{0,112},{16,0},{32,16},{48,32},{64,48},{80,64},{96,80},{112,96},{1... | collective-permute-start | bytes 14155784 | tf_op jit(solution)/shard_map/ppermute | solution.py:12
  186.3 102.5 %collective-permute-start.1 = (bf16[4,8,9,64,128]{4,1,3,2,0:T(8,128)(2,1)}, bf16[4,8,9,64,128]{4,1,3,2,0:T(8,128)(2,1)}, u32[]{:S(2)}, u32[]{:S(2)}) collective-permute-start(bf16[4,8,9,64,128]{4,1,3,2,0:T(8,128)(2,1)} %broadcast_select_fusion), channel_id=1, source_target_pairs={{0,96},{16,112},{32,0},{48,16},{64,32},{80,48},{96,64},{112,80},{1... | collective-permute-start | bytes 14155784 | tf_op jit(solution)/shard_map/ppermute | solution.py:12
  293.8 103.1 %collective-permute-start.2 = (bf16[4,8,9,64,128]{4,1,3,2,0:T(8,128)(2,1)}, bf16[4,8,9,64,128]{4,1,3,2,0:T(8,128)(2,1)}, u32[]{:S(2)}, u32[]{:S(2)}) collective-permute-start(bf16[4,8,9,64,128]{4,1,3,2,0:T(8,128)(2,1)} %broadcast_select_fusion.1), channel_id=1, source_target_pairs={{0,64},{16,80},{32,96},{48,112},{64,0},{80,16},{96,32},{112,48},{1... | collective-permute-start | bytes 14155784 | tf_op jit(solution)/shard_map/ppermute | solution.py:12
  295.3 218.5 %copy-start.29 = (f32[8,8]{1,0:T(8,128)S(1)}, f32[8,8]{1,0:T(8,128)}, u32[]{:S(2)}) copy-start(f32[8,8]{1,0:T(8,128)} %param.7) | copy-start | bytes 772
  399.8 2.2 copy-start.13
  402.0 105.2 %collective-permute-start.3 = (bf16[4,8,9,64,128]{4,1,3,2,0:T(8,128)(2,1)S(1)}, bf16[4,8,9,64,128]{4,1,3,2,0:T(8,128)(2,1)}, u32[]{:S(2)}, u32[]{:S(2)}) collective-permute-start(bf16[4,8,9,64,128]{4,1,3,2,0:T(8,128)(2,1)S(1)} %broadcast_select_fusion.2), channel_id=1, source_target_pairs={{0,112},{16,0},{32,16},{48,32},{64,48},{80,64},{96,80},{112,96},{1... | collective-permute-start | bytes 14155784 | tf_op jit(solution)/shard_map/ppermute | solution.py:12
  507.2 103.9 %collective-permute-start.4 = (bf16[4,8,9,64,128]{4,1,3,2,0:T(8,128)(2,1)}, bf16[4,8,9,64,128]{4,1,3,2,0:T(8,128)(2,1)}, u32[]{:S(2)}, u32[]{:S(2)}) collective-permute-start(bf16[4,8,9,64,128]{4,1,3,2,0:T(8,128)(2,1)} %collective-permute-done.3), channel_id=1, source_target_pairs={{0,112},{16,0},{32,16},{48,32},{64,48},{80,64},{96,80},{112,96},{1... | collective-permute-start | bytes 14155784 | tf_op jit(solution)/shard_map/ppermute | solution.py:12
  515.2 2.1 copy-start.27
  618.9 5.1 copy-start.2
  645.5 4.8 copy-start.5
  650.2 2.5 copy-start.4
  652.7 3.2 copy-start.3
  663.0 1.7 copy-start.26
  668.4 1.7 copy-start.24
  673.5 2.4 copy-start.10
  673.5 2.4 copy-start.21
  673.5 2.4 copy-start.22
  679.3 2.4 copy-start.8
  679.3 2.4 copy-start.19
  679.3 2.4 copy-start.20
  713.5 72.3 %copy-start.1 = (bf16[8,9,64,128]{3,2,1,0:T(8,128)(2,1)S(1)}, bf16[8,9,64,128]{3,2,1,0:T(8,128)(2,1)}, u32[]{:S(2)}) copy-start(bf16[8,9,64,128]{3,2,1,0:T(8,128)(2,1)} %param.6) | copy-start | bytes 3538948
  (14 other events, 19.7 us)
Sparse Core Ops, SparseCore 0:
  716.4 69.3 reduce-scatter.1
